TPU v7x, 32 devices: a whole 2x2x4 slice. The times are simulated.
32 devices in a mesh: groups: 2 (over y), frame: 4 (over z), query: 2 (over x), chan: 2 (over core).
Axes of the slice: x: 2, y: 2, z: 4, core: 2. Of those that a mesh axis runs over, the one named last changes fastest.
Arguments:
- features: bfloat16 [8, 64, 64, 256], P(('groups', 'frame'), None, None, 'chan'), parts along dimension 0, may hold values from -6 to 6
- query_frame: int32 [256], P(('groups', 'query')), parts along dimension 0, may hold values from 0 to 3
- query_pixel: int32 [256, 2], P(('groups', 'query')), parts along dimension 0, may hold values from 0 to 63
- conv_first: bfloat16 [3, 3, 1, 16], replicated, may hold values from -2 to 2
- conv_second: bfloat16 [3, 3, 16, 32], replicated, may hold values from -0.5 to 0.5
- depth_kernel: float32 [2, 3, 512], replicated, may hold values from -3 to 3
- w_in: bfloat16 [2, 2048, 512], P(None, ('frame', 'chan')), may hold values from -0.25 to 0.25
- w_out: bfloat16 [2, 2048, 512], P(None, ('frame', 'chan')), may hold values from -0.125 to 0.125
Outputs:
- tracks: bfloat16 [256, 4, 512], P(('groups', 'query'), 'frame'), parts along dimension 0
There are 2 independent parts, one for each index of `groups`. A program takes and returns all parts, laid end to end along the dimension named above; an argument that names none is the same for every part. Nothing has to cross between parts.
All inputs are finite; a program needn't handle non-finite values.
Results may differ from a plain program's by a relative error of at most 0.02.
Values may be sent and summed in bfloat16 or wider, within the bound.
A program may use at most 64 MiB of HBM per device.

v0:
```python
import math
import jax
import jax.numpy as jnp
from jax import lax
from jax.sharding import PartitionSpec as P

MIXERS = 2


def padded_2(block, sides, width):
    for axis, dim in sides:
        count = lax.axis_size(axis)
        forward = [(i, i + 1) for i in range(count - 1)]
        backward = [(target, source) for source, target in forward]
        low = lax.ppermute(
            lax.slice_in_dim(block, block.shape[dim] - width, None, axis=dim), axis, forward
        )
        high = lax.ppermute(lax.slice_in_dim(block, 0, width, axis=dim), axis, backward)
        block = jnp.concatenate([low, block, high], axis=dim)
    return block


def pool_maps(corr_maps, conv_first, conv_second):
    first_maps = lax.conv_general_dilated(
        corr_maps,
        conv_first,
        (2, 2),
        "SAME",
        dimension_numbers=("HWCN", "HWIO", "HWCN"),
        preferred_element_type=jnp.float32,
    )
    first_maps = jax.nn.relu(first_maps).astype(jnp.bfloat16)
    second_maps = lax.conv_general_dilated(
        first_maps,
        conv_second,
        (2, 2),
        "SAME",
        dimension_numbers=("HWCN", "HWIO", "HWCN"),
        preferred_element_type=jnp.float32,
    )
    second_maps = jax.nn.relu(second_maps)
    window = second_maps.shape[0] // 4
    pooled = second_maps.reshape(
        4, window, 4, window, second_maps.shape[2], second_maps.shape[3]
    ).mean(axis=(1, 3))
    return pooled.reshape(16 * second_maps.shape[2], second_maps.shape[3]).T


def layer_norm(state):
    centre = state - jnp.mean(state, axis=-1, keepdims=True)
    spread = jnp.mean(centre * centre, axis=-1, keepdims=True)
    return (centre * lax.rsqrt(spread + 1e-05)).astype(jnp.bfloat16)


def depth_mix(padded, kernel):
    length = padded.shape[1] - 2
    wide = padded.astype(jnp.float32)
    summed = (
        kernel[0] * wide[:, :length] + kernel[1] * wide[:, 1 : length + 1] + kernel[2] * wide[:, 2:]
    )
    return summed.astype(jnp.bfloat16)


def on_device(
    features, query_frame, query_pixel, conv_first, conv_second, depth_kernel, w_in, w_out
):
    frame_count = features.shape[0]
    side_cells = features.shape[1]
    chan_width = features.shape[3]
    row_ids = query_pixel[:, 0]
    col_ids = query_pixel[:, 1]
    local_frame = query_frame - lax.axis_index("frame") * frame_count
    owned_mask = ((local_frame >= 0) & (local_frame < frame_count)).astype(jnp.float32)
    picked = features[jnp.clip(local_frame, 0, frame_count - 1), row_ids, col_ids, :].astype(
        jnp.float32
    )
    picked = picked * owned_mask[:, None]
    query_vectors = lax.psum(picked.astype(jnp.bfloat16), "frame")
    corr_scale = 1.0 / math.sqrt(chan_width * lax.axis_size("chan"))
    flat = features.reshape(frame_count * side_cells * side_cells, chan_width)
    local_corr = jnp.dot(flat, query_vectors.T, preferred_element_type=jnp.float32)
    summed = lax.psum_scatter(
        local_corr.astype(jnp.bfloat16), "chan", scatter_dimension=1, tiled=True
    ).astype(jnp.float32)
    corr_maps = (
        (summed * corr_scale)
        .astype(jnp.bfloat16)
        .reshape(frame_count, side_cells, side_cells, 1, summed.shape[1])
    )
    pooled = lax.map(lambda frame_maps: pool_maps(frame_maps, conv_first, conv_second), corr_maps)
    state = jnp.transpose(pooled, (1, 0, 2))
    for mixer in range(MIXERS):
        normed = layer_norm(state)
        padded = padded_2(normed, (("frame", 1),), 1)
        mixed = depth_mix(padded, depth_kernel[mixer])
        row_block = mixed.reshape(-1, mixed.shape[2])
        empty = jnp.zeros(row_block.shape, jnp.float32)
        in_piece = lax.all_gather(w_in[mixer], ("frame", "chan"), axis=0, tiled=True)
        out_piece = lax.all_gather(w_out[mixer], ("frame", "chan"), axis=0, tiled=True)
        pre_act = lax.dot_general(
            row_block, in_piece, (((1,), (1,)), ((), ())), preferred_element_type=jnp.float32
        )
        hidden = jax.nn.gelu(pre_act, approximate=False).astype(jnp.bfloat16)
        update = empty + jnp.dot(hidden, out_piece, preferred_element_type=jnp.float32)
        state = state + update.reshape(state.shape)
    tracks = state.astype(jnp.bfloat16)
    tracks = lax.all_gather(tracks, "chan", axis=0, tiled=True)
    return tracks


def solution(mesh):
    in_specs = (
        P(("groups", "frame"), None, None, "chan"),
        P(("groups", "query")),
        P(("groups", "query"), None),
        P(),
        P(),
        P(),
        P(None, ("frame", "chan"), None),
        P(None, ("frame", "chan"), None),
    )
    out_specs = P(("groups", "query"), "frame", None)
    return jax.shard_map(
        on_device, mesh=mesh, in_specs=in_specs, out_specs=out_specs, check_vma=False
    )
```

profile of v0, /device:TPU:0, one launch (start us, length us, event | category | flops | bytes accessed | tf_op | source)
XLA Modules:
  0.0 164.9 jit_solution(18240802262996446110)
XLA Ops:
  7.4 0.0 copy-start
  7.4 0.0 copy-start.1
  7.4 0.0 copy-start.2
  7.4 0.0 reduce-scatter.2.cloned.1.call-start
  7.4 0.8 and_convert_fusion
  8.2 0.8 fusion.145
  9.0 0.0 copy-done
  9.0 0.8 gather_fusion
  9.8 0.1 multiply_convert_fusion.3
  9.9 20.5 %psum.7 = bf16[64,128]{1,0:T(8,128)(2,1)S(1)} all-reduce(bf16[64,128]{1,0:T(8,128)(2,1)S(1)} %multiply_convert_fusion.3), channel_id=1, replica_groups=mesh['groups'=2,'frame'=4,'query'=2,'chan'=2] {'frame'}, use_global_device_ids=true, to_apply=%region_0.1 | all-reduce | flops 8192 | bytes 32768 | tf_op jit(solution)/shard_map/psum | solution.py:78
  30.4 1.3 fusion
  31.7 0.0 reduce-scatter.2.cloned.1.call-update
  31.7 0.0 all-gather.10.cloned.1.call-start
  31.8 0.0 copy-done.1
  31.8 0.9 fusion.208
  32.6 0.0 all-gather.10.cloned.1.call-update
  32.6 0.0 all-gather.12.cloned.1.call-start
  32.7 0.0 copy-done.2
  32.7 0.8 fusion.209
  33.6 0.0 all-gather.12.cloned.1.call-update
  33.6 0.0 all-gather.14.cloned.1.call-start
  33.6 0.5 all-gather.14.cloned.1.call-update
  34.2 0.0 all-gather.16.cloned.1.call-start
  34.2 0.0 copy-start.4
  34.2 0.0 copy-start.5
  34.2 0.7 all-gather.16.cloned.1.call-update
  34.9 3.1 %reduce-scatter.2.cloned.1.call-done = bf16[4096,32]{0,1:T(8,128)(2,1)} async-done(((bf16[4096,64]{0,1:T(8,128)(2,1)}), bf16[4096,32]{0,1:T(8,128)(2,1)}) %reduce-scatter.2.cloned.1.call-update) | async-done | bytes 262160 | tf_op jit(solution)/shard_map/reduce_scatter | solution.py:82
  38.0 1.0 multiply_convert_fusion
  39.0 1.3 squeeze.21
  40.4 4.8 %copy.11 = bf16[64,64,1,32]{3,2,1,0:T(2,128)(2,1)S(1)} copy(bf16[64,64,1,32]{1,0,3,2:T(8,128)(2,1)} %squeeze.21) | data formatting | bytes 524288 | tf_op jit(solution)/shard_map/while/body/jit(dynamic_index_in_dim)/squeeze | solution.py:90
  45.1 0.0 copy-done.4
  45.1 0.0 copy-done.5
  45.2 8.0 %fusion.5 = f32[16,16,32,32]{2,3,1,0:T(8,128)} fusion(bf16[3,3,16,32]{3,2,1,0:T(8,128)(2,1)S(1)} %copy-done.4, bf16[64,64,1,32]{3,2,1,0:T(2,128)(2,1)S(1)} %copy.11, bf16[3,3,1,16]{3,1,2,0:T(4,128)(2,1)S(1)} %copy-done.5), kind=kOutput, calls=%fused_computation.7 | convolution fusion | flops 82936832 | bytes 1320224 | tf_op jit(solution)/shard_map/while/body/eval_jaxpr/conv_general_dilated | solution.py:33
  53.2 0.0 copy-start.3
  53.2 2.8 %reduce_sum.46 = f32[4,4,32,32]{2,3,1,0:T(8,128)S(1)} reduce(f32[4,4,4,4,32,32]{4,5,3,2,1,0:T(8,128)} %bitcast.79, f32[]{:T(128)} %constant.16.clone.1), dimensions={1,3}, to_apply=%region_2.3 | reduce | flops 245760 | bytes 1114116 | tf_op jit(solution)/shard_map/while/body/eval_jaxpr/reduce_sum | solution.py:45
  56.0 0.1 fusion.207
  56.1 0.2 copy.13
  56.3 0.2 div.19
  56.5 0.2 multiply_reduce_fusion.1
  56.7 0.1 fusion.117
  56.8 3.6 %collective-permute-start = (bf16[32,1,512]{2,0,1:T(8,128)(2,1)S(1)}, bf16[32,1,512]{2,0,1:T(8,128)(2,1)S(1)}, u32[]{:S(2)}, u32[]{:S(2)}) collective-permute-start(bf16[32,1,512]{2,0,1:T(8,128)(2,1)S(1)} %fusion.117), channel_id=1, source_target_pairs={{0,4},{4,8},{8,12},{1,5},{5,9},{9,13},{2,6},{6,10},{10,14},{3,7},{... | collective-permute-start | bytes 98312 | tf_op jit(solution)/shard_map/ppermute | solution.py:15
  60.4 1.3 collective-permute-start.1
  61.7 0.0 copy-done.3
  61.7 0.2 collective-permute-done
  62.0 4.2 %collective-permute-done.1 = bf16[32,1,512]{2,0,1:T(8,128)(2,1)S(1)} collective-permute-done((bf16[32,1,512]{2,0,1:T(8,128)(2,1)S(1)}, bf16[32,1,512]{2,0,1:T(8,128)(2,1)S(1)}, u32[]{:S(2)}, u32[]{:S(2)}) %collective-permute-start.1) | collective-permute-done | bytes 32800 | tf_op jit(solution)/shard_map/ppermute | solution.py:18
  66.2 0.0 all-gather.10.cloned.1.call-done
  66.2 24.8 %all-gather.12.cloned.1.call-done = bf16[1,2048,512]{2,1,0:T(8,128)(2,1)} async-done(((bf16[1,256,512]{2,1,0:T(8,128)(2,1)}), bf16[1,2048,512]{2,1,0:T(8,128)(2,1)}) %all-gather.12.cloned.1.call-update) | async-done | bytes 2097168 | tf_op jit(solution)/shard_map/all_gather | solution.py:99
  91.0 3.6 %fusion.211 = (f32[32]{0:T(128)S(1)}, f32[32,512]{1,0:T(8,128)S(1)}) fusion(bf16[1,2048,512]{2,1,0:T(8,128)(2,1)} %all-gather.12.cloned.1.call-done, bf16[1,2048,512]{2,1,0:T(8,128)(2,1)} %all-gather.10.cloned.1.call-done, f32[32,3,512]{2,0,1:T(8,128)S(1)} %maximum_convert_fusion.4, f32[512]{0:T(512)S(1)} %bitcast.84, f32[512]{0:T(512)S(1)} %bitcast.85, ...), kind=kOutput, calls=%fused_computation.229 | convolution fusion | flops 138608608 | bytes 4528256 | tf_op jit(solution)/shard_map/dot_general | solution.py:104
  94.6 0.2 multiply_reduce_fusion
  94.8 0.1 fusion.118
  94.9 3.3 %collective-permute-start.2 = (bf16[32,1,512]{2,0,1:T(8,128)(2,1)S(1)}, bf16[32,1,512]{2,0,1:T(8,128)(2,1)S(1)}, u32[]{:S(2)}, u32[]{:S(2)}) collective-permute-start(bf16[32,1,512]{2,0,1:T(8,128)(2,1)S(1)} %fusion.118), channel_id=1, source_target_pairs={{0,4},{4,8},{8,12},{1,5},{5,9},{9,13},{2,6},{6,10},{10,14},{3,7},{... | collective-permute-start | bytes 98312 | tf_op jit(solution)/shard_map/ppermute | solution.py:15
  98.3 1.3 collective-permute-start.3
  99.6 0.3 collective-permute-done.2
  99.8 5.6 %collective-permute-done.3 = bf16[32,1,512]{2,0,1:T(8,128)(2,1)S(1)} collective-permute-done((bf16[32,1,512]{2,0,1:T(8,128)(2,1)S(1)}, bf16[32,1,512]{2,0,1:T(8,128)(2,1)S(1)}, u32[]{:S(2)}, u32[]{:S(2)}) %collective-permute-start.3) | collective-permute-done | bytes 32800 | tf_op jit(solution)/shard_map/ppermute | solution.py:18
  105.5 16.5 %all-gather.14.cloned.1.call-done = bf16[1,2048,512]{2,1,0:T(8,128)(2,1)} async-done(((bf16[1,256,512]{2,1,0:T(8,128)(2,1)}), bf16[1,2048,512]{2,1,0:T(8,128)(2,1)}) %all-gather.14.cloned.1.call-update) | async-done | bytes 2097168 | tf_op jit(solution)/shard_map/all_gather | solution.py:98
  122.0 29.3 %all-gather.16.cloned.1.call-done = bf16[1,2048,512]{2,1,0:T(8,128)(2,1)} async-done(((bf16[1,256,512]{2,1,0:T(8,128)(2,1)}), bf16[1,2048,512]{2,1,0:T(8,128)(2,1)}) %all-gather.16.cloned.1.call-update) | async-done | bytes 2097168 | tf_op jit(solution)/shard_map/all_gather | solution.py:99
  151.3 3.5 %fusion.20 = bf16[32,512]{1,0:T(8,128)(2,1)S(1)} fusion(f32[32,512]{1,0:T(8,128)S(1)} %get-tuple-element.33, bf16[1,2048,512]{2,1,0:T(8,128)(2,1)} %all-gather.16.cloned.1.call-done, bf16[1,2048,512]{2,1,0:T(8,128)(2,1)} %all-gather.14.cloned.1.call-done, f32[32,3,512]{2,0,1:T(8,128)S(1)} %maximum_convert_fusion.5, f32[512]{0:T(512)S(1)} %bitcast.82, ...), kind=kOutput, calls=%fused_computation.18 | convolution fusion | flops 138608640 | bytes 4495360 | tf_op jit(solution)/shard_map/dot_general | solution.py:104
  154.8 1.9 %all-gather.4 = bf16[64,512]{1,0:T(8,128)(2,1)S(1)} all-gather(bf16[32,512]{1,0:T(8,128)(2,1)S(1)} %fusion.20), channel_id=6, replica_groups=mesh['groups'=2,'frame'=4,'query'=2,'chan'=2] {'chan'}, dimensions={0}, use_global_device_ids=true | all-gather | bytes 98304 | tf_op jit(solution)/shard_map/all_gather | solution.py:107
  156.7 0.6 copy.18
  (7 shorter events, 0.1 us)
Async XLA Ops:
  7.4 1.6 copy-start
  7.4 24.4 %copy-start.1 = (bf16[2,256,512]{2,1,0:T(8,128)(2,1)S(1)}, bf16[2,256,512]{2,1,0:T(8,128)(2,1)}, u32[]{:S(2)}) copy-start(bf16[2,256,512]{2,1,0:T(8,128)(2,1)} %param.14) | copy-start | bytes 1572868
  7.4 25.3 %copy-start.2 = (bf16[2,256,512]{2,1,0:T(8,128)(2,1)S(1)}, bf16[2,256,512]{2,1,0:T(8,128)(2,1)}, u32[]{:S(2)}) copy-start(bf16[2,256,512]{2,1,0:T(8,128)(2,1)} %param.15) | copy-start | bytes 1572868
  7.4 30.6 %reduce-scatter.2.cloned.1.call-start = ((), (), s32[]{:S(2)}) async-start(), calls=%async_computation.1 | async-start | bytes 786432 | tf_op jit(solution)/shard_map/reduce_scatter | solution.py:82
  31.7 34.5 %all-gather.10.cloned.1.call-start = ((), (), s32[]{:S(2)}) async-start(), calls=%async_computation.2 | async-start | bytes 2359296 | tf_op jit(solution)/shard_map/all_gather | solution.py:98
  32.6 58.4 %all-gather.12.cloned.1.call-start = ((), (), s32[]{:S(2)}) async-start(), calls=%async_computation.3 | async-start | bytes 2359296 | tf_op jit(solution)/shard_map/all_gather | solution.py:99
  33.6 88.4 %all-gather.14.cloned.1.call-start = ((), (), s32[]{:S(2)}) async-start(), calls=%async_computation.4 | async-start | bytes 2359296 | tf_op jit(solution)/shard_map/all_gather | solution.py:98
  34.2 117.2 %all-gather.16.cloned.1.call-start = ((), (), s32[]{:S(2)}) async-start(), calls=%async_computation.5 | async-start | bytes 2359296 | tf_op jit(solution)/shard_map/all_gather | solution.py:99
  34.2 10.9 %copy-start.4 = (bf16[3,3,16,32]{3,2,1,0:T(8,128)(2,1)S(1)}, bf16[3,3,16,32]{3,2,1,0:T(8,128)(2,1)}, u32[]{:S(2)}) copy-start(bf16[3,3,16,32]{3,2,1,0:T(8,128)(2,1)} %param.12) | copy-start | bytes 27652
  34.2 10.9 %copy-start.5 = (bf16[3,3,1,16]{3,1,2,0:T(4,128)(2,1)S(1)}, bf16[3,3,1,16]{3,1,2,0:T(4,128)(2,1)}, u32[]{:S(2)}) copy-start(bf16[3,3,1,16]{3,1,2,0:T(4,128)(2,1)} %param.11) | copy-start | bytes 868
  53.2 8.5 %copy-start.3 = (f32[2,3,512]{2,0,1:T(2,128)S(1)}, f32[2,3,512]{2,0,1:T(2,128)}, u32[]{:S(2)}) copy-start(f32[2,3,512]{2,0,1:T(2,128)} %param.13) | copy-start | bytes 36868
  56.8 5.2 %collective-permute-start = (bf16[32,1,512]{2,0,1:T(8,128)(2,1)S(1)}, bf16[32,1,512]{2,0,1:T(8,128)(2,1)S(1)}, u32[]{:S(2)}, u32[]{:S(2)}) collective-permute-start(bf16[32,1,512]{2,0,1:T(8,128)(2,1)S(1)} %fusion.117), channel_id=1, source_target_pairs={{0,4},{4,8},{8,12},{1,5},{5,9},{9,13},{2,6},{6,10},{10,14},{3,7},{... | collective-permute-start | bytes 98312 | tf_op jit(solution)/shard_map/ppermute | solution.py:15
  60.4 5.8 %collective-permute-start.1 = (bf16[32,1,512]{2,0,1:T(8,128)(2,1)S(1)}, bf16[32,1,512]{2,0,1:T(8,128)(2,1)S(1)}, u32[]{:S(2)}, u32[]{:S(2)}) collective-permute-start(bf16[32,1,512]{2,0,1:T(8,128)(2,1)S(1)} %fusion.117), channel_id=1, source_target_pairs={{4,0},{8,4},{12,8},{5,1},{9,5},{13,9},{6,2},{10,6},{14,10},{7,3},{... | collective-permute-start | bytes 98312 | tf_op jit(solution)/shard_map/ppermute | solution.py:18
  94.9 4.9 %collective-permute-start.2 = (bf16[32,1,512]{2,0,1:T(8,128)(2,1)S(1)}, bf16[32,1,512]{2,0,1:T(8,128)(2,1)S(1)}, u32[]{:S(2)}, u32[]{:S(2)}) collective-permute-start(bf16[32,1,512]{2,0,1:T(8,128)(2,1)S(1)} %fusion.118), channel_id=1, source_target_pairs={{0,4},{4,8},{8,12},{1,5},{5,9},{9,13},{2,6},{6,10},{10,14},{3,7},{... | collective-permute-start | bytes 98312 | tf_op jit(solution)/shard_map/ppermute | solution.py:15
  98.3 7.2 %collective-permute-start.3 = (bf16[32,1,512]{2,0,1:T(8,128)(2,1)S(1)}, bf16[32,1,512]{2,0,1:T(8,128)(2,1)S(1)}, u32[]{:S(2)}, u32[]{:S(2)}) collective-permute-start(bf16[32,1,512]{2,0,1:T(8,128)(2,1)S(1)} %fusion.118), channel_id=1, source_target_pairs={{4,0},{8,4},{12,8},{5,1},{9,5},{13,9},{6,2},{10,6},{14,10},{7,3},{... | collective-permute-start | bytes 98312 | tf_op jit(solution)/shard_map/ppermute | solution.py:18
Sparse Core Ops, SparseCore 0:
  31.8 6.1 reduce-scatter.1
Sparse Core Ops, SparseCore 1:
  33.8 27.3 all-gather.9
  62.6 28.4 all-gather.11
  92.5 29.5 all-gather.13
  123.6 27.6 all-gather.15
where the time goes:
time: 165 us
  waiting for transfers between devices  85.4 us (52%)
  blocking collectives  22.4 us (14%)
  matrix products  16.4 us (10%)
  between operations  15.3 us (9%)
  local copies, waits for them, and re-layouts  9.7 us (6%)
  starting transfers between devices  9.66 us (6%)
  other arithmetic  6.17 us (4%)
    all_gather x2, waiting for transfers between devices, on_device(): lax.all_gather(w_out[mixer], ('frame', 'chan'), axis=0, tiled=True)  54.1 us
    psum x1, blocking collectives, on_device(): query_vectors = lax.psum(picked.astype(jnp.bfloat16), 'frame')  20.5 us
    all_gather x2, waiting for transfers between devices, on_device(): lax.all_gather(w_in[mixer], ('frame', 'chan'), axis=0, tiled=True)  16.6 us
    ppermute x2, waiting for transfers between devices, padded_2(): lax.ppermute(lax.slice_in_dim(block, 0, width, axis=dim), axis, backward)  9.86 us
    conv_general_dilated x1, matrix products, pool_maps(): lax.conv_general_dilated(first_maps, conv_second, (2, 2), 'SAME', dimensi...  8.04 us
    dot_general x2, matrix products, on_device(): jnp.dot(hidden, out_piece, preferred_element_type=jnp.float32)  7.08 us
    ppermute x2, starting transfers between devices, padded_2(): lax.ppermute(lax.slice_in_dim(block, block.shape[dim] - width, None, axis...  6.9 us
    squeeze x2, local copies, waits for them, and re-layouts, on_device(): lax.map(lambda frame_maps: pool_maps(frame_maps, conv_first, conv_second)...  6.11 us
  transfers between devices with their start and end apart: 9, of which 8 were waited for; matrix products, arithmetic and copies ran while one was open for 15% of the time, Pallas kernels for 0%

commit v1 on v0

--- a/solution.py
+++ b/solution.py
@@ -1,3 +1,4 @@
+import functools
 import math
 import jax
 import jax.numpy as jnp
@@ -5,6 +6,16 @@
 from jax.sharding import PartitionSpec as P
 
 MIXERS = 2
+
+
+def rings_meet(unit, ax_name):
+    after = jnp.concatenate(
+        lax.all_to_all(jnp.stack([unit] * lax.axis_size(ax_name), 0), ax_name, 0, 0), 0
+    )
+    return after
+
+
+return_all_pairs_all = functools.partial(rings_meet, ax_name=("frame", "chan"))
 
 
 def padded_2(block, sides, width):
@@ -95,7 +106,7 @@
         mixed = depth_mix(padded, depth_kernel[mixer])
         row_block = mixed.reshape(-1, mixed.shape[2])
         empty = jnp.zeros(row_block.shape, jnp.float32)
-        in_piece = lax.all_gather(w_in[mixer], ("frame", "chan"), axis=0, tiled=True)
+        in_piece = return_all_pairs_all(w_in[mixer])
         out_piece = lax.all_gather(w_out[mixer], ("frame", "chan"), axis=0, tiled=True)
         pre_act = lax.dot_general(
             row_block, in_piece, (((1,), (1,)), ((), ())), preferred_element_type=jnp.float32

time: 165 us -> 202 us (1.22)
  starting transfers between devices: 9.66 us -> 31.1 us
  waiting for transfers between devices: 85.4 us -> 98.6 us
  local copies, waits for them, and re-layouts: 9.7 us -> 12.4 us
    all_to_all x0 -> x2, waiting for transfers between devices: none -> 82.1 us  [rings_meet(): lax.all_to_all(jnp.stack([unit] * lax.axis_size(ax_name), 0), ax_name, 0, 0)]
    all_gather x2, waiting for transfers between devices: 54.1 us -> 0.05 us  [on_device(): lax.all_gather(w_out[mixer], ('frame', 'chan'), axis=0, tiled=True)]
    all_gather x2 -> x0, waiting for transfers between devices: 16.6 us -> none  [on_device(): lax.all_gather(w_in[mixer], ('frame', 'chan'), axis=0, tiled=True)]
    ppermute x2, starting transfers between devices: 6.9 us -> 20.4 us  [padded_2(): lax.ppermute(lax.slice_in_dim(block, block.shape[dim] - width, None, axis...]
    ppermute x2, waiting for transfers between devices: 0.53 us -> 11.7 us  [padded_2(): lax.ppermute(lax.slice_in_dim(block, block.shape[dim] - width, None, axis...]
    all_to_all x0 -> x2, starting transfers between devices: none -> 7.98 us  [rings_meet(): lax.all_to_all(jnp.stack([unit] * lax.axis_size(ax_name), 0), ax_name, 0, 0)]
    ppermute x2, waiting for transfers between devices: 9.86 us -> 4.23 us  [padded_2(): lax.ppermute(lax.slice_in_dim(block, 0, width, axis=dim), axis, backward)]
    another operation x0 -> x2, local copies, waits for them, and re-layouts: none -> 3.19 us  [rings_meet(): jnp.stack([unit] * lax.axis_size(ax_name), 0)]
  transfers between devices with their start and end apart: 9 -> 9, of which waited for: 8 -> 4; matrix products, arithmetic and copies ran while one was open for 15% -> 13% of each run, Pallas kernels for 0% -> 0%
where the time goes in v1:
time: 202 us
  waiting for transfers between devices  98.6 us (49%)
  starting transfers between devices  31.1 us (15%)
  blocking collectives  22.4 us (11%)
  matrix products  15.8 us (8%)
  between operations  15.1 us (7%)
  local copies, waits for them, and re-layouts  12.4 us (6%)
  other arithmetic  6.25 us (3%)
    all_to_all x2, waiting for transfers between devices, rings_meet(): lax.all_to_all(jnp.stack([unit] * lax.axis_size(ax_name), 0), ax_name, 0, 0)  82.1 us
    psum x1, blocking collectives, on_device(): query_vectors = lax.psum(picked.astype(jnp.bfloat16), 'frame')  20.5 us
    ppermute x2, starting transfers between devices, padded_2(): lax.ppermute(lax.slice_in_dim(block, block.shape[dim] - width, None, axis...  20.4 us
    ppermute x2, waiting for transfers between devices, padded_2(): lax.ppermute(lax.slice_in_dim(block, block.shape[dim] - width, None, axis...  11.7 us
    conv_general_dilated x1, matrix products, pool_maps(): lax.conv_general_dilated(first_maps, conv_second, (2, 2), 'SAME', dimensi...  8.04 us
    all_to_all x2, starting transfers between devices, rings_meet(): lax.all_to_all(jnp.stack([unit] * lax.axis_size(ax_name), 0), ax_name, 0, 0)  7.98 us
    dot_general x2, matrix products, on_device(): jnp.dot(hidden, out_piece, preferred_element_type=jnp.float32)  6.46 us
    squeeze x2, local copies, waits for them, and re-layouts, on_device(): lax.map(lambda frame_maps: pool_maps(frame_maps, conv_first, conv_second)...  6.11 us
  transfers between devices with their start and end apart: 9, of which 4 were waited for; matrix products, arithmetic and copies ran while one was open for 13% of the time, Pallas kernels for 0%

profile of v1, /device:TPU:0, one launch (start us, length us, event | category | flops | bytes accessed | tf_op | source)
XLA Modules:
  0.0 201.6 jit_solution(2781545342387816600)
XLA Ops:
  7.4 0.0 copy-start
  7.4 0.0 copy-start.3
  7.4 0.0 copy-start.4
  7.4 0.0 reduce-scatter.2.cloned.1.call-start
  7.4 0.8 and_convert_fusion
  8.2 0.8 fusion.143
  9.0 0.0 copy-done
  9.0 0.8 gather_fusion
  9.8 0.1 multiply_convert_fusion.3
  9.9 20.5 %psum.7 = bf16[64,128]{1,0:T(8,128)(2,1)S(1)} all-reduce(bf16[64,128]{1,0:T(8,128)(2,1)S(1)} %multiply_convert_fusion.3), channel_id=1, replica_groups=mesh['groups'=2,'frame'=4,'query'=2,'chan'=2] {'frame'}, use_global_device_ids=true, to_apply=%region_0.1 | all-reduce | flops 8192 | bytes 32768 | tf_op jit(solution)/shard_map/psum | solution.py:89
  30.4 1.3 fusion
  31.7 0.0 reduce-scatter.2.cloned.1.call-update
  31.7 0.0 all-gather.6.cloned.1.call-start
  31.8 0.0 copy-done.3
  31.8 0.8 fusion.206
  32.6 0.0 all-gather.6.cloned.1.call-update
  32.6 0.0 copy-done.4
  32.7 1.5 stack.6
  34.2 3.6 %all-to-all-start = ((bf16[8,256,512]{2,1,0:T(8,128)(2,1)}), bf16[8,256,512]{2,1,0:T(8,128)(2,1)S(1)}, u32[]{:S(2)}, u32[]{:S(2)}) async-start(bf16[8,256,512]{2,1,0:T(8,128)(2,1)} %stack.6), calls=%async_computation.1 | async-start | bytes 4194304 | tf_op jit(solution)/shard_map/all_to_all | solution.py:13
  37.8 0.0 all-gather.8.cloned.1.call-start
  37.9 0.5 all-gather.8.cloned.1.call-update
  38.4 82.1 %all-to-all-done = bf16[8,256,512]{2,1,0:T(8,128)(2,1)S(1)} async-done(((bf16[8,256,512]{2,1,0:T(8,128)(2,1)}), bf16[8,256,512]{2,1,0:T(8,128)(2,1)S(1)}, u32[]{:S(2)}, u32[]{:S(2)}) %all-to-all-start) | async-done | bytes 2097184 | tf_op jit(solution)/shard_map/all_to_all | solution.py:13
  120.5 0.0 copy-start.1
  120.5 1.7 stack.7
  122.2 0.3 copy-done.1
  122.5 4.4 %all-to-all-start.1 = ((bf16[8,256,512]{2,1,0:T(8,128)(2,1)}), bf16[8,256,512]{2,1,0:T(8,128)(2,1)}, u32[]{:S(2)}, u32[]{:S(2)}) async-start(bf16[8,256,512]{2,1,0:T(8,128)(2,1)} %stack.7), calls=%async_computation.2 | async-start | bytes 4194304 | tf_op jit(solution)/shard_map/all_to_all | solution.py:13
  126.9 0.0 copy-start.6
  126.9 0.0 copy-start.7
  126.9 0.0 reduce-scatter.2.cloned.1.call-done
  127.0 1.0 multiply_convert_fusion
  127.9 1.3 squeeze.15
  129.3 4.8 %copy.11 = bf16[64,64,1,32]{3,2,1,0:T(2,128)(2,1)S(1)} copy(bf16[64,64,1,32]{1,0,3,2:T(8,128)(2,1)} %squeeze.15) | data formatting | bytes 524288 | tf_op jit(solution)/shard_map/while/body/jit(dynamic_index_in_dim)/squeeze | solution.py:101
  134.1 0.0 copy-done.6
  134.1 0.0 copy-done.7
  134.1 8.0 %fusion.5 = f32[16,16,32,32]{2,3,1,0:T(8,128)} fusion(bf16[3,3,16,32]{3,2,1,0:T(8,128)(2,1)S(1)} %copy-done.6, bf16[64,64,1,32]{3,2,1,0:T(2,128)(2,1)S(1)} %copy.11, bf16[3,3,1,16]{3,1,2,0:T(4,128)(2,1)S(1)} %copy-done.7), kind=kOutput, calls=%fused_computation.7 | convolution fusion | flops 82936832 | bytes 1320224 | tf_op jit(solution)/shard_map/while/body/eval_jaxpr/conv_general_dilated | solution.py:44
  142.1 0.0 copy-start.5
  142.1 0.0 copy-start.2
  142.1 2.9 %reduce_sum.46 = f32[4,4,32,32]{2,3,1,0:T(8,128)S(1)} reduce(f32[4,4,4,4,32,32]{4,5,3,2,1,0:T(8,128)} %bitcast.77, f32[]{:T(128)} %constant.16.clone.1), dimensions={1,3}, to_apply=%region_2.3 | reduce | flops 245760 | bytes 1114116 | tf_op jit(solution)/shard_map/while/body/eval_jaxpr/reduce_sum | solution.py:56
  145.0 0.1 fusion.205
  145.2 0.2 copy.13
  145.3 0.2 div.19
  145.5 0.2 multiply_reduce_fusion.1
  145.7 0.1 fusion.107
  145.8 3.8 %collective-permute-start = (bf16[32,1,512]{2,0,1:T(8,128)(2,1)S(1)}, bf16[32,1,512]{2,0,1:T(8,128)(2,1)S(1)}, u32[]{:S(2)}, u32[]{:S(2)}) collective-permute-start(bf16[32,1,512]{2,0,1:T(8,128)(2,1)S(1)} %fusion.107), channel_id=1, source_target_pairs={{0,4},{4,8},{8,12},{1,5},{5,9},{9,13},{2,6},{6,10},{10,14},{3,7},{... | collective-permute-start | bytes 98312 | tf_op jit(solution)/shard_map/ppermute | solution.py:26
  149.6 1.3 collective-permute-start.1
  150.9 0.0 copy-done.5
  150.9 11.4 %collective-permute-done = bf16[32,1,512]{2,0,1:T(8,128)(2,1)S(1)} collective-permute-done((bf16[32,1,512]{2,0,1:T(8,128)(2,1)S(1)}, bf16[32,1,512]{2,0,1:T(8,128)(2,1)S(1)}, u32[]{:S(2)}, u32[]{:S(2)}) %collective-permute-start) | collective-permute-done | bytes 32800 | tf_op jit(solution)/shard_map/ppermute | solution.py:26
  162.4 0.0 collective-permute-done.1
  162.4 0.0 all-gather.6.cloned.1.call-done
  162.4 0.0 copy-done.2
  162.4 3.0 %fusion.208 = (f32[32]{0:T(128)S(1)}, f32[32,512]{1,0:T(8,128)S(1)}) fusion(bf16[1,2048,512]{2,1,0:T(8,128)(2,1)} %all-gather.6.cloned.1.call-done, bf16[2048,512]{1,0:T(8,128)(2,1)S(1)} %bitcast.78, f32[32,3,512]{2,0,1:T(8,128)S(1)} %maximum_convert_fusion.4, f32[512]{0:T(512)S(1)} %bitcast.83, f32[512]{0:T(512)S(1)} %bitcast.84, f32[512]{0:T(512)S(1)} %bitcast.85, ...), kind=kOutput, calls=%fused_computation.228 | convolution fusion | flops 138608608 | bytes 4528256 | tf_op jit(solution)/shard_map/dot_general | solution.py:115
  165.4 0.2 multiply_reduce_fusion
  165.6 0.1 fusion.108
  165.7 16.6 %collective-permute-start.2 = (bf16[32,1,512]{2,0,1:T(8,128)(2,1)S(1)}, bf16[32,1,512]{2,0,1:T(8,128)(2,1)S(1)}, u32[]{:S(2)}, u32[]{:S(2)}) collective-permute-start(bf16[32,1,512]{2,0,1:T(8,128)(2,1)S(1)} %fusion.108), channel_id=1, source_target_pairs={{0,4},{4,8},{8,12},{1,5},{5,9},{9,13},{2,6},{6,10},{10,14},{3,7},{... | collective-permute-start | bytes 98312 | tf_op jit(solution)/shard_map/ppermute | solution.py:26
  182.3 1.3 collective-permute-start.3
  183.6 0.3 collective-permute-done.2
  183.9 4.2 %collective-permute-done.3 = bf16[32,1,512]{2,0,1:T(8,128)(2,1)S(1)} collective-permute-done((bf16[32,1,512]{2,0,1:T(8,128)(2,1)S(1)}, bf16[32,1,512]{2,0,1:T(8,128)(2,1)S(1)}, u32[]{:S(2)}, u32[]{:S(2)}) %collective-permute-start.3) | collective-permute-done | bytes 32800 | tf_op jit(solution)/shard_map/ppermute | solution.py:29
  188.2 0.0 all-to-all-done.1
  188.2 0.0 all-gather.8.cloned.1.call-done
  188.2 3.5 %fusion.16 = bf16[32,512]{1,0:T(8,128)(2,1)S(1)} fusion(f32[32,512]{1,0:T(8,128)S(1)} %get-tuple-element.33, bf16[1,2048,512]{2,1,0:T(8,128)(2,1)} %all-gather.8.cloned.1.call-done, bf16[2048,512]{1,0:T(8,128)(2,1)} %bitcast.20, f32[32,3,512]{2,0,1:T(8,128)S(1)} %maximum_convert_fusion.5, f32[512]{0:T(512)S(1)} %bitcast.81, f32[512]{0:T(512)S(1)} %bitcast.82, ...), kind=kOutput, calls=%fused_computation.14 | convolution fusion | flops 138608640 | bytes 4495360 | tf_op jit(solution)/shard_map/dot_general | solution.py:115
  191.7 1.9 all-gather.2
  193.6 0.6 copy.18
  (8 shorter events, 0.1 us)
Async XLA Ops:
  7.4 1.6 copy-start
  7.4 24.4 %copy-start.3 = (bf16[2,256,512]{2,1,0:T(8,128)(2,1)S(1)}, bf16[2,256,512]{2,1,0:T(8,128)(2,1)}, u32[]{:S(2)}) copy-start(bf16[2,256,512]{2,1,0:T(8,128)(2,1)} %param.15) | copy-start | bytes 1572868
  7.4 25.3 %copy-start.4 = (bf16[2,256,512]{2,1,0:T(8,128)(2,1)S(1)}, bf16[2,256,512]{2,1,0:T(8,128)(2,1)}, u32[]{:S(2)}) copy-start(bf16[2,256,512]{2,1,0:T(8,128)(2,1)} %param.14) | copy-start | bytes 1572868
  7.4 119.6 %reduce-scatter.2.cloned.1.call-start = ((), (), s32[]{:S(2)}) async-start(), calls=%async_computation.3 | async-start | bytes 786432 | tf_op jit(solution)/shard_map/reduce_scatter | solution.py:93
  31.7 130.7 %all-gather.6.cloned.1.call-start = ((), (), s32[]{:S(2)}) async-start(), calls=%async_computation.4 | async-start | bytes 2359296 | tf_op jit(solution)/shard_map/all_gather | solution.py:110
  34.2 86.3 %all-to-all-start = ((bf16[8,256,512]{2,1,0:T(8,128)(2,1)}), bf16[8,256,512]{2,1,0:T(8,128)(2,1)S(1)}, u32[]{:S(2)}, u32[]{:S(2)}) async-start(bf16[8,256,512]{2,1,0:T(8,128)(2,1)} %stack.6), calls=%async_computation.1 | async-start | bytes 4194304 | tf_op jit(solution)/shard_map/all_to_all | solution.py:13
  37.8 150.4 %all-gather.8.cloned.1.call-start = ((), (), s32[]{:S(2)}) async-start(), calls=%async_computation.5 | async-start | bytes 2359296 | tf_op jit(solution)/shard_map/all_gather | solution.py:110
  120.5 2.0 %copy-start.1 = (bf16[8,256,512]{2,1,0:T(8,128)(2,1)}, bf16[8,256,512]{2,1,0:T(8,128)(2,1)S(1)}, u32[]{:S(2)}) copy-start(bf16[8,256,512]{2,1,0:T(8,128)(2,1)S(1)} %all-to-all-done) | copy-start | bytes 6291460
  122.5 65.7 %all-to-all-start.1 = ((bf16[8,256,512]{2,1,0:T(8,128)(2,1)}), bf16[8,256,512]{2,1,0:T(8,128)(2,1)}, u32[]{:S(2)}, u32[]{:S(2)}) async-start(bf16[8,256,512]{2,1,0:T(8,128)(2,1)} %stack.7), calls=%async_computation.2 | async-start | bytes 4194304 | tf_op jit(solution)/shard_map/all_to_all | solution.py:13
  126.9 7.2 %copy-start.6 = (bf16[3,3,16,32]{3,2,1,0:T(8,128)(2,1)S(1)}, bf16[3,3,16,32]{3,2,1,0:T(8,128)(2,1)}, u32[]{:S(2)}) copy-start(bf16[3,3,16,32]{3,2,1,0:T(8,128)(2,1)} %param.12) | copy-start | bytes 27652
  126.9 7.2 %copy-start.7 = (bf16[3,3,1,16]{3,1,2,0:T(4,128)(2,1)S(1)}, bf16[3,3,1,16]{3,1,2,0:T(4,128)(2,1)}, u32[]{:S(2)}) copy-start(bf16[3,3,1,16]{3,1,2,0:T(4,128)(2,1)} %param.11) | copy-start | bytes 868
  142.1 8.8 %copy-start.5 = (f32[2,3,512]{2,0,1:T(2,128)S(1)}, f32[2,3,512]{2,0,1:T(2,128)}, u32[]{:S(2)}) copy-start(f32[2,3,512]{2,0,1:T(2,128)} %param.13) | copy-start | bytes 36868
  142.1 20.3 %copy-start.2 = (bf16[8,256,512]{2,1,0:T(8,128)(2,1)S(1)}, bf16[8,256,512]{2,1,0:T(8,128)(2,1)}, u32[]{:S(2)}) copy-start(bf16[8,256,512]{2,1,0:T(8,128)(2,1)} %copy-done.1) | copy-start | bytes 6291460
  145.8 16.5 %collective-permute-start = (bf16[32,1,512]{2,0,1:T(8,128)(2,1)S(1)}, bf16[32,1,512]{2,0,1:T(8,128)(2,1)S(1)}, u32[]{:S(2)}, u32[]{:S(2)}) collective-permute-start(bf16[32,1,512]{2,0,1:T(8,128)(2,1)S(1)} %fusion.107), channel_id=1, source_target_pairs={{0,4},{4,8},{8,12},{1,5},{5,9},{9,13},{2,6},{6,10},{10,14},{3,7},{... | collective-permute-start | bytes 98312 | tf_op jit(solution)/shard_map/ppermute | solution.py:26
  149.6 12.8 %collective-permute-start.1 = (bf16[32,1,512]{2,0,1:T(8,128)(2,1)S(1)}, bf16[32,1,512]{2,0,1:T(8,128)(2,1)S(1)}, u32[]{:S(2)}, u32[]{:S(2)}) collective-permute-start(bf16[32,1,512]{2,0,1:T(8,128)(2,1)S(1)} %fusion.107), channel_id=1, source_target_pairs={{4,0},{8,4},{12,8},{5,1},{9,5},{13,9},{6,2},{10,6},{14,10},{7,3},{... | collective-permute-start | bytes 98312 | tf_op jit(solution)/shard_map/ppermute | solution.py:29
  165.7 18.2 %collective-permute-start.2 = (bf16[32,1,512]{2,0,1:T(8,128)(2,1)S(1)}, bf16[32,1,512]{2,0,1:T(8,128)(2,1)S(1)}, u32[]{:S(2)}, u32[]{:S(2)}) collective-permute-start(bf16[32,1,512]{2,0,1:T(8,128)(2,1)S(1)} %fusion.108), channel_id=1, source_target_pairs={{0,4},{4,8},{8,12},{1,5},{5,9},{9,13},{2,6},{6,10},{10,14},{3,7},{... | collective-permute-start | bytes 98312 | tf_op jit(solution)/shard_map/ppermute | solution.py:26
  182.3 5.8 %collective-permute-start.3 = (bf16[32,1,512]{2,0,1:T(8,128)(2,1)S(1)}, bf16[32,1,512]{2,0,1:T(8,128)(2,1)S(1)}, u32[]{:S(2)}, u32[]{:S(2)}) collective-permute-start(bf16[32,1,512]{2,0,1:T(8,128)(2,1)S(1)} %fusion.108), channel_id=1, source_target_pairs={{4,0},{8,4},{12,8},{5,1},{9,5},{13,9},{6,2},{10,6},{14,10},{7,3},{... | collective-permute-start | bytes 98312 | tf_op jit(solution)/shard_map/ppermute | solution.py:29
Sparse Core Ops, SparseCore 0:
  31.8 6.1 reduce-scatter.1
Sparse Core Ops, SparseCore 1:
  33.8 44.3 all-gather.5
  79.6 42.0 all-gather.7
